TPU v7x, 32 devices: a whole 2x2x4 slice. The times are simulated.
32 devices in a mesh: dom: 16 (over z, x, core), band: 2 (over y).
Axes of the slice: x: 2, y: 2, z: 4, core: 2. Of those that a mesh axis runs over, the one named last changes fastest.
Arguments:
- wavefun: float32 [13824, 512], P('dom', 'band')
- cell_ops: float32 [64, 343, 343], P('dom'), as said below
- cell_map: int32 [64, 343], P('dom'), may hold values from 0 to 1007, as said below
- face_list: int32 [2304], P('dom'), may hold values from 0 to 863, as said below
Outputs:
- ortho_bands: float32 [13824, 512], P('dom', 'band')
Inputs may be any that keep to these rules, and one draw needn't show every extreme that they name: `cell_map`: each row lists the 343 distinct local numbers of a cell's nodes; a number below 864 is a node of the cell's own domain, 864 + j stands for the j-th lower face node of the next domain (periodic over domains); every node of a domain belongs to some cell of that domain. `face_list`: the 144 entries of each domain are distinct node numbers of that domain. `cell_ops`: each cell's matrix is symmetric.
All inputs are finite; a program needn't handle non-finite values.
Results may differ from a plain program's by a relative error of at most 0.0001.
Values sent between devices are 32-bit elements; how exact they have to be, the bound alone decides.
A program may use at most 64 MiB of HBM per device.

v0:
```python
import jax
import jax.numpy as jnp
from jax import lax
from jax.sharding import PartitionSpec as P

DEGREE = 2
cheb_centre = 1.0
cheb_half = 1.6


def shifted(block, axis, distance):
    devices = range(lax.axis_size(axis))
    route = [((i - distance) % len(devices), i) for i in devices]
    return lax.ppermute(block, axis, route)


def on_device(wavefun, cell_ops, cell_map, face_list):
    owned_rows = wavefun.shape[0]
    block_width = wavefun.shape[1]
    flat_map = cell_map.reshape(-1)

    def local_apply(extended):
        cell_values = extended[flat_map].reshape(cell_map.shape[0], cell_map.shape[1], block_width)
        products = jnp.einsum(
            "cij,cjb->cib", cell_ops, cell_values, precision=lax.Precision.HIGHEST
        )
        return jnp.zeros_like(extended).at[flat_map].add(products.reshape(-1, block_width))

    def operate(vector):
        fetched = shifted(vector[face_list], "dom", -1)
        applied = local_apply(jnp.concatenate([vector, fetched], 0))
        returned = shifted(applied[owned_rows:], "dom", 1)
        return applied[:owned_rows].at[face_list].add(returned)

    latest = (operate(wavefun) - cheb_centre * wavefun) / cheb_half

    def advance(counter, carried):
        earlier, current = carried
        following = 2.0 * (operate(current) - cheb_centre * current) / cheb_half - earlier
        return (current, following)

    earlier, latest = lax.fori_loop(1, DEGREE, advance, (wavefun, latest))
    full_bands = lax.all_gather(latest, "band", axis=1, tiled=True)
    partial_value = jnp.einsum("nb,nc->bc", full_bands, full_bands, precision=lax.Precision.HIGHEST)
    margin = lax.psum(partial_value, "dom")
    norm_value = jnp.sqrt(jnp.sum(margin * margin) + 1e-06)
    full_width = margin.shape[0]
    offset = lax.axis_index("band") * block_width
    scaled_cols = lax.dynamic_slice_in_dim(margin, offset, block_width, 1) / norm_value
    identity_cols = lax.dynamic_slice_in_dim(
        jnp.eye(full_width, dtype=jnp.float32), offset, block_width, 1
    )
    mixing = (3.0 * identity_cols - scaled_cols) / 2.0
    return jnp.dot(full_bands, mixing, precision=lax.Precision.HIGHEST)


def solution(mesh):
    return jax.shard_map(
        on_device,
        mesh=mesh,
        in_specs=(P("dom", "band"), P("dom", None, None), P("dom", None), P("dom")),
        out_specs=P("dom", "band"),
        check_vma=False,
    )
```

profile of v0, /device:TPU:0, one launch (start us, length us, event | category | flops | bytes accessed | tf_op | source)
XLA Modules:
  0.0 234.2 jit_solution(618638592340945098)
XLA Ops:
  6.5 0.0 copy-start
  6.5 0.0 all-gather.2.cloned.1.call-start
  6.5 0.8 compare_select_fusion.1
  7.4 2.0 gather_fusion
  9.3 5.5 %collective-permute-start = (f32[144,256]{1,0:T(8,128)S(1)}, f32[144,256]{1,0:T(8,128)S(1)}, u32[]{:S(2)}, u32[]{:S(2)}) collective-permute-start(f32[144,256]{1,0:T(8,128)S(1)} %gather_fusion), channel_id=1, source_target_pairs={{2,0},{4,2},{6,4},{8,6},{10,8},{12,10},{14,12},{16,14},{18,16},{20... | collective-permute-start | bytes 442376 | tf_op jit(solution)/shard_map/ppermute | solution.py:14
  14.8 0.8 reshape.45
  15.7 1.9 collective-permute-done
  17.5 1.2 pad_maximum_fusion
  18.7 4.6 %gather_fusion.1 = f32[1372,256]{1,0:T(8,128)} fusion(f32[1008,256]{1,0:T(8,128)S(1)} %pad_maximum_fusion, s32[2048]{0:T(1024)S(1)} %pad_clamp_fusion), kind=kCustom, calls=%fused_computation.1 | custom fusion | bytes 2815344 | tf_op jit(solution)/shard_map/gather | solution.py:23
  23.3 1.5 reshape.46
  24.8 0.0 copy-done
  24.8 3.7 %fusion.4 = f32[4,343,256]{2,1,0:T(8,128)} fusion(f32[4,343,256]{2,1,0:T(8,128)S(1)} %reshape.46, f32[4,343,343]{2,0,1:T(4,128)S(1)} %copy-done), kind=kOutput, calls=%fused_computation.12 | convolution fusion | flops 1445670912 | bytes 4692240 | tf_op jit(solution)/shard_map/cij,cjb->cib/dot_general | solution.py:24
  28.5 2.6 %reshape.86 = f32[1372,256]{1,0:T(8,128)} reshape(f32[4,343,256]{2,1,0:T(8,128)} %fusion.4) | data formatting | bytes 2809856 | tf_op jit(solution)/shard_map/reshape | solution.py:27
  31.1 8.7 %scatter_custom_fusion = f32[1008,256]{1,0:T(8,128)S(1)} fusion(s32[1372]{0:T(1024)S(1)} %fusion.25, f32[1372,256]{1,0:T(8,128)} %reshape.86, f32[]{:T(128)} %constant.12.clone.1), kind=kCustom, calls=%fused_computation.29 | custom fusion | flops 351232 | bytes 1032704 | tf_op jit(solution)/shard_map/scatter-add | solution.py:27
  39.9 0.0 copy-start.3
  39.9 1.0 copy-done.3
  40.8 0.0 collective-permute-start.1
  40.9 1.2 slice.26
  42.1 6.2 %collective-permute-done.1 = f32[144,256]{1,0:T(8,128)S(1)} collective-permute-done((f32[144,256]{1,0:T(8,128)S(1)}, f32[144,256]{1,0:T(8,128)S(1)}, u32[]{:S(2)}, u32[]{:S(2)}) %collective-permute-start.1) | collective-permute-done | bytes 147488 | tf_op jit(solution)/shard_map/ppermute | solution.py:14
  48.3 1.7 scatter_fusion
  50.0 0.0 copy-start.1
  50.0 2.6 %subtract_multiply_fusion = f32[864,256]{1,0:T(8,128)} fusion(f32[864,256]{1,0:T(8,128)S(1)} %scatter_fusion, f32[864,256]{1,0:T(8,128)} %param.4), kind=kLoop, calls=%fused_computation.18 | loop fusion | flops 442368 | bytes 2654208 | tf_op jit(solution)/shard_map/div | solution.py:35
  52.5 2.0 gather_fusion.2
  54.5 0.0 copy-done.1
  54.5 0.2 collective-permute-start.2
  54.8 2.7 %collective-permute-done.2 = f32[144,256]{1,0:T(8,128)S(1)} collective-permute-done((f32[144,256]{1,0:T(8,128)S(1)}, f32[144,256]{1,0:T(8,128)S(1)}, u32[]{:S(2)}, u32[]{:S(2)}) %collective-permute-start.2) | collective-permute-done | bytes 147488 | tf_op jit(solution)/shard_map/while/body/eval_jaxpr/ppermute | solution.py:14
  57.4 1.2 pad_maximum_fusion.1
  58.7 4.6 %gather_fusion.3 = f32[1372,256]{1,0:T(8,128)} fusion(f32[1008,256]{1,0:T(8,128)S(1)} %pad_maximum_fusion.1, s32[2048]{0:T(1024)S(1)} %pad_clamp_fusion), kind=kCustom, calls=%fused_computation.3 | custom fusion | bytes 2815344 | tf_op jit(solution)/shard_map/while/body/eval_jaxpr/gather | solution.py:23
  63.2 1.5 reshape.48
  64.7 3.7 %fusion.7 = f32[4,343,256]{2,1,0:T(8,128)} fusion(f32[4,343,256]{2,1,0:T(8,128)S(1)} %reshape.48, f32[4,343,343]{2,0,1:T(4,128)S(1)} %copy-done), kind=kOutput, calls=%fused_computation.13 | convolution fusion | flops 1445670912 | bytes 4692240 | tf_op jit(solution)/shard_map/while/body/eval_jaxpr/cij,cjb->cib/dot_general | solution.py:24
  68.4 2.6 %reshape.102 = f32[1372,256]{1,0:T(8,128)} reshape(f32[4,343,256]{2,1,0:T(8,128)} %fusion.7) | data formatting | bytes 2809856 | tf_op jit(solution)/shard_map/while/body/eval_jaxpr/reshape | solution.py:27
  71.0 8.7 %scatter_custom_fusion.2 = f32[1008,256]{1,0:T(8,128)S(1)} fusion(s32[1372]{0:T(1024)S(1)} %fusion.25, f32[1372,256]{1,0:T(8,128)} %reshape.102, f32[]{:T(128)} %constant.12.clone.1), kind=kCustom, calls=%fused_computation.27 | custom fusion | flops 351232 | bytes 1032704 | tf_op jit(solution)/shard_map/while/body/eval_jaxpr/scatter-add | solution.py:27
  79.8 0.1 collective-permute-start.3
  79.8 1.0 slice.28
  80.8 0.0 copy-start.2
  80.8 6.4 %collective-permute-done.3 = f32[144,256]{1,0:T(8,128)S(1)} collective-permute-done((f32[144,256]{1,0:T(8,128)S(1)}, f32[144,256]{1,0:T(8,128)S(1)}, u32[]{:S(2)}, u32[]{:S(2)}) %collective-permute-start.3) | collective-permute-done | bytes 147488 | tf_op jit(solution)/shard_map/while/body/eval_jaxpr/ppermute | solution.py:14
  87.3 3.3 %scatter_fusion.1 = f32[864,256]{1,0:T(8,128)} fusion(f32[864,256]{1,0:T(8,128)} %slice.28, s32[144]{0:T(256)S(1)} %compare_select_fusion.1, f32[144,256]{1,0:T(8,128)S(1)} %collective-permute-done.3), kind=kCustom, calls=%fused_computation.7 | custom fusion | flops 36864 | bytes 442944 | tf_op jit(solution)/shard_map/while/body/eval_jaxpr/scatter-add | solution.py:33
  90.6 0.0 copy-done.2
  90.6 2.6 %multiply_subtract_fusion = f32[864,256]{1,0:T(8,128)} fusion(f32[864,256]{1,0:T(8,128)} %param.4, f32[864,256]{1,0:T(8,128)} %scatter_fusion.1, f32[864,256]{1,0:T(8,128)S(1)} %copy-done.2), kind=kLoop, calls=%fused_computation.17 | loop fusion | flops 1105920 | bytes 3538944 | tf_op jit(solution)/shard_map/while/body/eval_jaxpr/sub | solution.py:39
  93.2 0.0 all-gather.2.cloned.1.call-update
  93.2 0.3 all-reduce.2.cloned.1.call-start
  93.5 26.6 %all-gather.2.cloned.1.call-done = f32[864,512]{1,0:T(8,128)} async-done(((f32[864,256]{1,0:T(8,128)}), f32[864,512]{1,0:T(8,128)}) %all-gather.2.cloned.1.call-update) | async-done | bytes 1769488 | tf_op jit(solution)/shard_map/all_gather | solution.py:43
  120.0 6.5 %fusion.29 = f32[512,512]{1,0:T(8,128)} fusion(f32[864,512]{1,0:T(8,128)} %all-gather.2.cloned.1.call-done), kind=kOutput, calls=%fused_computation.43 | convolution fusion | flops 2717908992 | bytes 2818048 | tf_op jit(solution)/shard_map/nb,nc->bc/dot_general | solution.py:44
  126.6 0.0 all-reduce.2.cloned.1.call-update
  126.6 93.8 %all-reduce.2.cloned.1.call-done = f32[512,512]{1,0:T(8,128)} async-done(((f32[512,512]{1,0:T(8,128)}), f32[512,512]{1,0:T(8,128)}) %all-reduce.2.cloned.1.call-update) | async-done | bytes 1048592 | tf_op jit(solution)/shard_map/psum | solution.py:45
  220.5 2.1 multiply_reduce_fusion
  223.2 4.1 %fusion.10 = f32[864,256]{1,0:T(8,128)} fusion(f32[864,512]{1,0:T(8,128)} %all-gather.2.cloned.1.call-done, f32[512,512]{1,0:T(8,128)} %all-reduce.2.cloned.1.call-done, s32[]{:T(128)S(6)} %select_n.27, f32[]{:T(128)S(6)} %sqrt.3), kind=kOutput, calls=%fused_computation.20 | convolution fusion | flops 1359872000 | bytes 3180032 | tf_op jit(solution)/shard_map/dot_general | solution.py:54
  (5 shorter events, 0.1 us)
Async XLA Ops:
  6.5 18.3 %copy-start = (f32[4,343,343]{2,0,1:T(4,128)S(1)}, f32[4,343,343]{2,0,1:T(4,128)}, u32[]{:S(2)}) copy-start(f32[4,343,343]{2,0,1:T(4,128)} %param.5) | copy-start | bytes 5647156
  6.5 113.5 %all-gather.2.cloned.1.call-start = ((), (), s32[]{:S(2)}) async-start(), calls=%async_computation | async-start | bytes 2654208 | tf_op jit(solution)/shard_map/all_gather | solution.py:43
  9.3 8.2 %collective-permute-start = (f32[144,256]{1,0:T(8,128)S(1)}, f32[144,256]{1,0:T(8,128)S(1)}, u32[]{:S(2)}, u32[]{:S(2)}) collective-permute-start(f32[144,256]{1,0:T(8,128)S(1)} %gather_fusion), channel_id=1, source_target_pairs={{2,0},{4,2},{6,4},{8,6},{10,8},{12,10},{14,12},{16,14},{18,16},{20... | collective-permute-start | bytes 442376 | tf_op jit(solution)/shard_map/ppermute | solution.py:14
  39.9 1.0 copy-start.3
  40.8 7.4 %collective-permute-start.1 = (f32[144,256]{1,0:T(8,128)S(1)}, f32[144,256]{1,0:T(8,128)S(1)}, u32[]{:S(2)}, u32[]{:S(2)}) collective-permute-start(f32[144,256]{1,0:T(8,128)S(1)} %slice.27), channel_id=1, source_target_pairs={{30,0},{0,2},{2,4},{4,6},{6,8},{8,10},{10,12},{12,14},{14,16},{16,... | collective-permute-start | bytes 442376 | tf_op jit(solution)/shard_map/ppermute | solution.py:14
  50.0 4.5 %copy-start.1 = (f32[864,256]{1,0:T(8,128)}, f32[864,256]{1,0:T(8,128)S(1)}, u32[]{:S(2)}) copy-start(f32[864,256]{1,0:T(8,128)S(1)} %scatter_fusion) | copy-start | bytes 2654212
  54.5 2.9 %collective-permute-start.2 = (f32[144,256]{1,0:T(8,128)S(1)}, f32[144,256]{1,0:T(8,128)S(1)}, u32[]{:S(2)}, u32[]{:S(2)}) collective-permute-start(f32[144,256]{1,0:T(8,128)S(1)} %gather_fusion.2), channel_id=1, source_target_pairs={{2,0},{4,2},{6,4},{8,6},{10,8},{12,10},{14,12},{16,14},{18,16},{20... | collective-permute-start | bytes 442376 | tf_op jit(solution)/shard_map/while/body/eval_jaxpr/ppermute | solution.py:14
  79.8 7.5 %collective-permute-start.3 = (f32[144,256]{1,0:T(8,128)S(1)}, f32[144,256]{1,0:T(8,128)S(1)}, u32[]{:S(2)}, u32[]{:S(2)}) collective-permute-start(f32[144,256]{1,0:T(8,128)S(1)} %slice.29), channel_id=1, source_target_pairs={{30,0},{0,2},{2,4},{4,6},{6,8},{8,10},{10,12},{12,14},{14,16},{16,... | collective-permute-start | bytes 442376 | tf_op jit(solution)/shard_map/while/body/eval_jaxpr/ppermute | solution.py:14
  80.8 9.8 %copy-start.2 = (f32[864,256]{1,0:T(8,128)S(1)}, f32[864,256]{1,0:T(8,128)}, u32[]{:S(2)}) copy-start(f32[864,256]{1,0:T(8,128)} %copy-done.1) | copy-start | bytes 2654212
  93.2 127.3 %all-reduce.2.cloned.1.call-start = ((), (), s32[]{:S(2)}) async-start(), calls=%async_computation.1 | async-start | bytes 2097152 | tf_op jit(solution)/shard_map/psum | solution.py:45
Sparse Core Ops, SparseCore 0:
  93.3 26.6 all-gather.1
  126.7 93.6 all-reduce.1
where the time goes:
time: 235 us; the launch traced here: 234 us
  waiting for transfers between devices  138 us (59%)
  other arithmetic  33.1 us (14%)
  local copies, waits for them, and re-layouts  25.3 us (11%)
  matrix products  18 us (8%)
  between operations  14.2 us (6%)
  starting transfers between devices  6.06 us (3%)
    psum x1, waiting for transfers between devices, on_device(): margin = lax.psum(partial_value, 'dom')  93.8 us
    all_gather x1, waiting for transfers between devices, on_device(): full_bands = lax.all_gather(latest, 'band', axis=1, tiled=True)  26.6 us
    scatter-add x2, other arithmetic, local_apply(): jnp.zeros_like(extended).at[flat_map].add(products.reshape(-1, block_width))  17.4 us
    ppermute x4, waiting for transfers between devices, shifted(): return lax.ppermute(block, axis, route)  17.1 us
    gather x2, local copies, waits for them, and re-layouts, local_apply(): extended[flat_map]  9.14 us
    dot_general x2, matrix products, local_apply(): jnp.einsum('cij,cjb->cib', cell_ops, cell_values, precision=lax.Precision...  7.36 us
    dot_general x1, matrix products, on_device(): jnp.einsum('nb,nc->bc', full_bands, full_bands, precision=lax.Precision.H...  6.54 us
    ppermute x4, starting transfers between devices, shifted(): return lax.ppermute(block, axis, route)  5.8 us
  transfers between devices with their start and end apart: 6, of which 6 were waited for; matrix products, arithmetic and copies ran while one was open for 1% of the time, Pallas kernels for 0%

commit v1 on v0

--- a/solution.py
+++ b/solution.py
@@ -42,7 +42,7 @@
     earlier, latest = lax.fori_loop(1, DEGREE, advance, (wavefun, latest))
     full_bands = lax.all_gather(latest, "band", axis=1, tiled=True)
     partial_value = jnp.einsum("nb,nc->bc", full_bands, full_bands, precision=lax.Precision.HIGHEST)
-    margin = lax.psum(partial_value, "dom")
+    margin = jnp.sum(lax.all_gather(partial_value, "dom"), axis=0)
     norm_value = jnp.sqrt(jnp.sum(margin * margin) + 1e-06)
     full_width = margin.shape[0]
     offset = lax.axis_index("band") * block_width

time: 235 us -> 274 us (1.17)
  waiting for transfers between devices: 138 us -> 170 us
  other arithmetic: 33.1 us -> 39.8 us
    all_gather x0 -> x1, waiting for transfers between devices: none -> 127 us  [on_device(): margin = jnp.sum(lax.all_gather(partial_value, 'dom'), axis=0)]
    psum x1 -> x0, waiting for transfers between devices: 93.8 us -> none  [on_device(): margin = lax.psum(partial_value, 'dom')]
    reduce_sum x0 -> x1, other arithmetic: none -> 7.95 us  [on_device(): margin = jnp.sum(lax.all_gather(partial_value, 'dom'), axis=0)]
where the time goes in v1:
time: 274 us; the launch traced here: 273 us
  waiting for transfers between devices  170 us (62%)
  other arithmetic  39.8 us (15%)
  local copies, waits for them, and re-layouts  25.3 us (9%)
  matrix products  17.8 us (6%)
  between operations  14.2 us (5%)
  starting transfers between devices  6.06 us (2%)
    all_gather x1, waiting for transfers between devices, on_device(): margin = jnp.sum(lax.all_gather(partial_value, 'dom'), axis=0)  127 us
    all_gather x1, waiting for transfers between devices, on_device(): full_bands = lax.all_gather(latest, 'band', axis=1, tiled=True)  26.6 us
    scatter-add x2, other arithmetic, local_apply(): jnp.zeros_like(extended).at[flat_map].add(products.reshape(-1, block_width))  17.4 us
    ppermute x4, waiting for transfers between devices, shifted(): return lax.ppermute(block, axis, route)  17.1 us
    gather x2, local copies, waits for them, and re-layouts, local_apply(): extended[flat_map]  9.14 us
    reduce_sum x1, other arithmetic, on_device(): margin = jnp.sum(lax.all_gather(partial_value, 'dom'), axis=0)  7.95 us
    dot_general x2, matrix products, local_apply(): jnp.einsum('cij,cjb->cib', cell_ops, cell_values, precision=lax.Precision...  7.36 us
    dot_general x1, matrix products, on_device(): jnp.einsum('nb,nc->bc', full_bands, full_bands, precision=lax.Precision.H...  6.48 us
  transfers between devices with their start and end apart: 6, of which 6 were waited for; matrix products, arithmetic and copies ran while one was open for 1% of the time, Pallas kernels for 0%

profile of v1, /device:TPU:0, one launch (start us, length us, event | category | flops | bytes accessed | tf_op | source)
XLA Modules:
  0.0 273.5 jit_solution(15837022647197267030)
XLA Ops:
  6.5 0.0 copy-start
  6.5 0.0 all-gather.4.cloned.1.call-start
  6.5 0.8 compare_select_fusion.1
  7.4 2.0 gather_fusion
  9.3 5.5 %collective-permute-start = (f32[144,256]{1,0:T(8,128)S(1)}, f32[144,256]{1,0:T(8,128)S(1)}, u32[]{:S(2)}, u32[]{:S(2)}) collective-permute-start(f32[144,256]{1,0:T(8,128)S(1)} %gather_fusion), channel_id=1, source_target_pairs={{2,0},{4,2},{6,4},{8,6},{10,8},{12,10},{14,12},{16,14},{18,16},{20... | collective-permute-start | bytes 442376 | tf_op jit(solution)/shard_map/ppermute | solution.py:14
  14.8 0.8 reshape.45
  15.7 1.9 collective-permute-done
  17.5 1.2 pad_maximum_fusion
  18.7 4.6 %gather_fusion.1 = f32[1372,256]{1,0:T(8,128)} fusion(f32[1008,256]{1,0:T(8,128)S(1)} %pad_maximum_fusion, s32[2048]{0:T(1024)S(1)} %pad_clamp_fusion), kind=kCustom, calls=%fused_computation.1 | custom fusion | bytes 2815344 | tf_op jit(solution)/shard_map/gather | solution.py:23
  23.3 1.5 reshape.46
  24.8 0.0 copy-done
  24.8 3.7 %fusion.4 = f32[4,343,256]{2,1,0:T(8,128)} fusion(f32[4,343,256]{2,1,0:T(8,128)S(1)} %reshape.46, f32[4,343,343]{2,0,1:T(4,128)S(1)} %copy-done), kind=kOutput, calls=%fused_computation.12 | convolution fusion | flops 1445670912 | bytes 4692240 | tf_op jit(solution)/shard_map/cij,cjb->cib/dot_general | solution.py:24
  28.5 2.6 reshape.86
  31.1 8.7 %scatter_custom_fusion = f32[1008,256]{1,0:T(8,128)S(1)} fusion(s32[1372]{0:T(1024)S(1)} %fusion.25, f32[1372,256]{1,0:T(8,128)} %reshape.86, f32[]{:T(128)} %constant.12.clone.1), kind=kCustom, calls=%fused_computation.29 | custom fusion | flops 351232 | bytes 1032704 | tf_op jit(solution)/shard_map/scatter-add | solution.py:27
  39.9 0.0 copy-start.3
  39.9 1.0 copy-done.3
  40.8 0.0 collective-permute-start.1
  40.9 1.2 slice.26
  42.1 6.2 %collective-permute-done.1 = f32[144,256]{1,0:T(8,128)S(1)} collective-permute-done((f32[144,256]{1,0:T(8,128)S(1)}, f32[144,256]{1,0:T(8,128)S(1)}, u32[]{:S(2)}, u32[]{:S(2)}) %collective-permute-start.1) | collective-permute-done | bytes 147488 | tf_op jit(solution)/shard_map/ppermute | solution.py:14
  48.3 1.7 scatter_fusion
  50.0 0.0 copy-start.1
  50.0 2.6 subtract_multiply_fusion
  52.5 2.0 gather_fusion.2
  54.5 0.0 copy-done.1
  54.5 0.2 collective-permute-start.2
  54.8 2.7 collective-permute-done.2
  57.4 1.2 pad_maximum_fusion.1
  58.7 4.6 %gather_fusion.3 = f32[1372,256]{1,0:T(8,128)} fusion(f32[1008,256]{1,0:T(8,128)S(1)} %pad_maximum_fusion.1, s32[2048]{0:T(1024)S(1)} %pad_clamp_fusion), kind=kCustom, calls=%fused_computation.3 | custom fusion | bytes 2815344 | tf_op jit(solution)/shard_map/while/body/eval_jaxpr/gather | solution.py:23
  63.2 1.5 reshape.48
  64.7 3.7 %fusion.7 = f32[4,343,256]{2,1,0:T(8,128)} fusion(f32[4,343,256]{2,1,0:T(8,128)S(1)} %reshape.48, f32[4,343,343]{2,0,1:T(4,128)S(1)} %copy-done), kind=kOutput, calls=%fused_computation.13 | convolution fusion | flops 1445670912 | bytes 4692240 | tf_op jit(solution)/shard_map/while/body/eval_jaxpr/cij,cjb->cib/dot_general | solution.py:24
  68.4 2.6 reshape.102
  71.0 8.7 %scatter_custom_fusion.2 = f32[1008,256]{1,0:T(8,128)S(1)} fusion(s32[1372]{0:T(1024)S(1)} %fusion.25, f32[1372,256]{1,0:T(8,128)} %reshape.102, f32[]{:T(128)} %constant.12.clone.1), kind=kCustom, calls=%fused_computation.27 | custom fusion | flops 351232 | bytes 1032704 | tf_op jit(solution)/shard_map/while/body/eval_jaxpr/scatter-add | solution.py:27
  79.8 0.1 collective-permute-start.3
  79.8 1.0 slice.28
  80.8 0.0 copy-start.2
  80.8 6.4 %collective-permute-done.3 = f32[144,256]{1,0:T(8,128)S(1)} collective-permute-done((f32[144,256]{1,0:T(8,128)S(1)}, f32[144,256]{1,0:T(8,128)S(1)}, u32[]{:S(2)}, u32[]{:S(2)}) %collective-permute-start.3) | collective-permute-done | bytes 147488 | tf_op jit(solution)/shard_map/while/body/eval_jaxpr/ppermute | solution.py:14
  87.3 3.3 %scatter_fusion.1 = f32[864,256]{1,0:T(8,128)} fusion(f32[864,256]{1,0:T(8,128)} %slice.28, s32[144]{0:T(256)S(1)} %compare_select_fusion.1, f32[144,256]{1,0:T(8,128)S(1)} %collective-permute-done.3), kind=kCustom, calls=%fused_computation.7 | custom fusion | flops 36864 | bytes 442944 | tf_op jit(solution)/shard_map/while/body/eval_jaxpr/scatter-add | solution.py:33
  90.6 0.0 copy-done.2
  90.6 2.6 multiply_subtract_fusion
  93.2 0.0 all-gather.4.cloned.1.call-update
  93.2 0.3 all-gather.6.cloned.1.call-start
  93.5 26.6 %all-gather.4.cloned.1.call-done = f32[864,512]{1,0:T(8,128)} async-done(((f32[864,256]{1,0:T(8,128)}), f32[864,512]{1,0:T(8,128)}) %all-gather.4.cloned.1.call-update) | async-done | bytes 1769488 | tf_op jit(solution)/shard_map/all_gather | solution.py:43
  120.0 6.5 %fusion.29 = f32[512,512]{1,0:T(8,128)} fusion(f32[864,512]{1,0:T(8,128)} %all-gather.4.cloned.1.call-done), kind=kOutput, calls=%fused_computation.43 | convolution fusion | flops 2717908992 | bytes 2818048 | tf_op jit(solution)/shard_map/nb,nc->bc/dot_general | solution.py:44
  126.5 0.0 all-gather.6.cloned.1.call-update
  126.5 126.6 %all-gather.6.cloned.1.call-done = f32[8192,512]{1,0:T(8,128)} async-done(((f32[512,512]{1,0:T(8,128)}), f32[8192,512]{1,0:T(8,128)}) %all-gather.6.cloned.1.call-update) | async-done | bytes 16777232 | tf_op jit(solution)/shard_map/all_gather | solution.py:45
  253.1 8.0 %reduce_sum.18 = f32[512,512]{1,0:T(8,128)S(1)} reduce(f32[16,512,512]{2,1,0:T(8,128)} %bitcast.10, f32[]{:T(128)} %constant.12.clone.1), dimensions={0}, to_apply=%region_4.5 | reduce | flops 3932160 | bytes 17825796 | tf_op jit(solution)/shard_map/reduce_sum | solution.py:45
  261.1 0.9 multiply_reduce_fusion
  262.6 4.0 %fusion.10 = f32[864,256]{1,0:T(8,128)} fusion(f32[864,512]{1,0:T(8,128)} %all-gather.4.cloned.1.call-done, f32[512,512]{1,0:T(8,128)S(1)} %reduce_sum.18, s32[]{:T(128)S(6)} %select_n.27, f32[]{:T(128)S(6)} %sqrt.3), kind=kOutput, calls=%fused_computation.20 | convolution fusion | flops 1359872000 | bytes 3180032 | tf_op jit(solution)/shard_map/dot_general | solution.py:54
  (5 shorter events, 0.1 us)
Async XLA Ops:
  6.5 18.3 %copy-start = (f32[4,343,343]{2,0,1:T(4,128)S(1)}, f32[4,343,343]{2,0,1:T(4,128)}, u32[]{:S(2)}) copy-start(f32[4,343,343]{2,0,1:T(4,128)} %param.5) | copy-start | bytes 5647156
  6.5 113.5 %all-gather.4.cloned.1.call-start = ((), (), s32[]{:S(2)}) async-start(), calls=%async_computation | async-start | bytes 2654208 | tf_op jit(solution)/shard_map/all_gather | solution.py:43
  9.3 8.2 %collective-permute-start = (f32[144,256]{1,0:T(8,128)S(1)}, f32[144,256]{1,0:T(8,128)S(1)}, u32[]{:S(2)}, u32[]{:S(2)}) collective-permute-start(f32[144,256]{1,0:T(8,128)S(1)} %gather_fusion), channel_id=1, source_target_pairs={{2,0},{4,2},{6,4},{8,6},{10,8},{12,10},{14,12},{16,14},{18,16},{20... | collective-permute-start | bytes 442376 | tf_op jit(solution)/shard_map/ppermute | solution.py:14
  39.9 1.0 copy-start.3
  40.8 7.4 %collective-permute-start.1 = (f32[144,256]{1,0:T(8,128)S(1)}, f32[144,256]{1,0:T(8,128)S(1)}, u32[]{:S(2)}, u32[]{:S(2)}) collective-permute-start(f32[144,256]{1,0:T(8,128)S(1)} %slice.27), channel_id=1, source_target_pairs={{30,0},{0,2},{2,4},{4,6},{6,8},{8,10},{10,12},{12,14},{14,16},{16,... | collective-permute-start | bytes 442376 | tf_op jit(solution)/shard_map/ppermute | solution.py:14
  50.0 4.5 %copy-start.1 = (f32[864,256]{1,0:T(8,128)}, f32[864,256]{1,0:T(8,128)S(1)}, u32[]{:S(2)}) copy-start(f32[864,256]{1,0:T(8,128)S(1)} %scatter_fusion) | copy-start | bytes 2654212
  54.5 2.9 %collective-permute-start.2 = (f32[144,256]{1,0:T(8,128)S(1)}, f32[144,256]{1,0:T(8,128)S(1)}, u32[]{:S(2)}, u32[]{:S(2)}) collective-permute-start(f32[144,256]{1,0:T(8,128)S(1)} %gather_fusion.2), channel_id=1, source_target_pairs={{2,0},{4,2},{6,4},{8,6},{10,8},{12,10},{14,12},{16,14},{18,16},{20... | collective-permute-start | bytes 442376 | tf_op jit(solution)/shard_map/while/body/eval_jaxpr/ppermute | solution.py:14
  79.8 7.5 %collective-permute-start.3 = (f32[144,256]{1,0:T(8,128)S(1)}, f32[144,256]{1,0:T(8,128)S(1)}, u32[]{:S(2)}, u32[]{:S(2)}) collective-permute-start(f32[144,256]{1,0:T(8,128)S(1)} %slice.29), channel_id=1, source_target_pairs={{30,0},{0,2},{2,4},{4,6},{6,8},{8,10},{10,12},{12,14},{14,16},{16,... | collective-permute-start | bytes 442376 | tf_op jit(solution)/shard_map/while/body/eval_jaxpr/ppermute | solution.py:14
  80.8 9.8 %copy-start.2 = (f32[864,256]{1,0:T(8,128)S(1)}, f32[864,256]{1,0:T(8,128)}, u32[]{:S(2)}) copy-start(f32[864,256]{1,0:T(8,128)} %copy-done.1) | copy-start | bytes 2654212
  93.2 159.9 %all-gather.6.cloned.1.call-start = ((), (), s32[]{:S(2)}) async-start(), calls=%async_computation.1 | async-start | bytes 17825792 | tf_op jit(solution)/shard_map/all_gather | solution.py:45
Sparse Core Ops, SparseCore 0:
  93.3 26.6 all-gather.3
  126.7 126.4 all-gather.5
